TPU v7x, 256 devices: a whole 4x4x8 slice. The times are simulated.
256 devices in a mesh: seq: 8 (over z_hi, x), exp: 32 (over z_lo, y, core).
Axes of the slice: x: 4, y: 4, z: 8 (z_hi: 2, z_lo: 4; z = z_hi * 4 + z_lo), core: 2. Of those that a mesh axis runs over, the one named last changes fastest.
Arguments:
- tokens: bfloat16 [8192, 1664], P('seq'), may hold values from -6 to 6
- out_grad: bfloat16 [8192, 1664], P('seq'), may hold values from -6 to 6
- slot_params: bfloat16 [1024, 1664], P('exp'), may hold values from -6 to 6
- first_mixing: float32 [64, 4, 4, 4], P('exp'), may hold values from -3 to 3
- first_blocks: bfloat16 [64, 4, 416, 2048], P('exp', None, None, 'seq'), may hold values from -0.15625 to 0.15625
- second_mixing: float32 [64, 4, 4, 4], P('exp'), may hold values from -3 to 3
- second_blocks: bfloat16 [64, 4, 2048, 416], P('exp', None, 'seq'), may hold values from -0.0625 to 0.0625
Outputs:
- grad_tokens: float32 [8192, 1664], P(('seq', 'exp'))
- grad_slots: float32 [1024, 1664], P('exp')
- grad_first_mixing: float32 [64, 4, 4, 4], P('exp')
- grad_first_blocks: bfloat16 [64, 4, 416, 2048], P('exp', None, None, 'seq')
- grad_second_mixing: float32 [64, 4, 4, 4], P('exp')
- grad_second_blocks: bfloat16 [64, 4, 2048, 416], P('exp', None, 'seq')
All inputs are finite; a program needn't handle non-finite values.
Results may differ from a plain program's by a relative error of at most 0.04.
Values may be sent and summed in bfloat16 or wider, within the bound.
No kernel may reach another device: no remote copies, remote signals or barrier semaphores. Data moves between devices by JAX's collectives and lax.ppermute only.
A program may use at most 128 MiB of HBM per device.

v0:
```python
import jax
import jax.numpy as jnp
from jax import lax
from jax.sharding import PartitionSpec as P

logit_gain = 64.0
norm_eps = 1e-06
gelu_coef = 0.7978845608028654
cubic_coef = 0.044715


def gelu_pair(preact):
    inner_arg = gelu_coef * (preact + cubic_coef * preact * preact * preact)
    tangent = jnp.tanh(inner_arg)
    output = 0.5 * preact * (1.0 + tangent)
    slopes = 0.5 * (1.0 + tangent) + 0.5 * preact * (1.0 - tangent * tangent) * gelu_coef * (
        1.0 + 3.0 * cubic_coef * preact * preact
    )
    return (output, slopes)


def mix_blocks(blocks, mixing):
    return jnp.einsum("sak,iab->sbik", blocks.astype(jnp.float32), mixing)


def expert_forward(slot_in, first_mixing, first_blocks, second_mixing, second_blocks):
    slots_here, model_width = slot_in.shape
    factors = first_mixing.shape[0]
    inner_width = model_width // factors
    hidden_block = first_blocks.shape[2]
    first_flat = (
        mix_blocks(slot_in.reshape(slots_here, factors, inner_width), first_mixing)
        .astype(jnp.bfloat16)
        .reshape(slots_here * factors, factors * inner_width)
    )
    preact = jnp.dot(
        first_flat,
        first_blocks.reshape(factors * inner_width, hidden_block),
        preferred_element_type=jnp.float32,
    ).reshape(slots_here, factors, hidden_block)
    activated, slopes = gelu_pair(preact)
    hidden = activated.astype(jnp.bfloat16)
    second_flat = (
        mix_blocks(hidden, second_mixing)
        .astype(jnp.bfloat16)
        .reshape(slots_here * factors, factors * hidden_block)
    )
    slot_out = jnp.dot(
        second_flat,
        second_blocks.reshape(factors * hidden_block, inner_width),
        preferred_element_type=jnp.float32,
    ).reshape(slots_here, model_width)
    return (slot_out, first_flat, hidden, slopes, second_flat)


def expert_backward(
    slot_in,
    grad_out,
    first_flat,
    hidden,
    slopes,
    second_flat,
    first_mixing,
    first_blocks,
    second_mixing,
    second_blocks,
):
    slots_here, model_width = slot_in.shape
    factors = first_mixing.shape[0]
    inner_width = model_width // factors
    hidden_block = first_blocks.shape[2]
    first_matrix = first_blocks.reshape(factors * inner_width, hidden_block)
    second_matrix = second_blocks.reshape(factors * hidden_block, inner_width)
    grad_rows = grad_out.reshape(slots_here * factors, inner_width)
    grad_second_in = jnp.dot(
        grad_rows, second_matrix.T, preferred_element_type=jnp.float32
    ).reshape(slots_here, factors, factors, hidden_block)
    grad_second_blocks = (
        jnp.dot(second_flat.T, grad_rows, preferred_element_type=jnp.float32)
        .astype(jnp.bfloat16)
        .reshape(factors, hidden_block, inner_width)
    )
    grad_second_mixing = jnp.einsum("sak,sbik->iab", hidden.astype(jnp.float32), grad_second_in)
    grad_hidden = jnp.einsum("iab,sbik->sak", second_mixing, grad_second_in)
    grad_preact = (
        (grad_hidden * slopes).astype(jnp.bfloat16).reshape(slots_here * factors, hidden_block)
    )
    grad_first_in = jnp.dot(
        grad_preact, first_matrix.T, preferred_element_type=jnp.float32
    ).reshape(slots_here, factors, factors, inner_width)
    grad_first_blocks = (
        jnp.dot(first_flat.T, grad_preact, preferred_element_type=jnp.float32)
        .astype(jnp.bfloat16)
        .reshape(factors, inner_width, hidden_block)
    )
    slot_split = slot_in.reshape(slots_here, factors, inner_width).astype(jnp.float32)
    grad_first_mixing = jnp.einsum("sad,sbid->iab", slot_split, grad_first_in)
    grad_slot = jnp.einsum("iab,sbid->sad", first_mixing, grad_first_in).reshape(
        slots_here, model_width
    )
    return (grad_slot, grad_first_mixing, grad_first_blocks, grad_second_mixing, grad_second_blocks)


def token_total(partial_sums):
    return lax.psum(partial_sums, "exp")


def slot_total(first_part, second_part):
    return lax.psum((first_part, second_part), "seq")


def unit_grad(unit_rows, unit_grad_rows, norms):
    return (
        unit_grad_rows - unit_rows * jnp.sum(unit_rows * unit_grad_rows, axis=1, keepdims=True)
    ) / norms


def local(tokens, out_grad, slot_params, first_mixing, first_blocks, second_mixing, second_blocks):
    token_values = tokens.astype(jnp.float32)
    token_norm = jnp.sqrt(jnp.sum(token_values * token_values, axis=1, keepdims=True) + norm_eps)
    token_unit = token_values / token_norm
    token_unit_b = token_unit.astype(jnp.bfloat16)
    slot_values = slot_params.astype(jnp.float32)
    slot_norm = jnp.sqrt(jnp.sum(slot_values * slot_values, axis=1, keepdims=True) + norm_eps)
    slot_unit = slot_values / slot_norm
    slot_unit_b = slot_unit.astype(jnp.bfloat16)
    logits = logit_gain * jnp.einsum(
        "sd,td->st", slot_unit_b, token_unit_b, preferred_element_type=jnp.float32
    )
    weights = jnp.exp(logits)
    input_part = jnp.dot(weights.astype(jnp.bfloat16), tokens, preferred_element_type=jnp.float32)
    combine_total = token_total(jnp.sum(weights, axis=0))
    input_sum, dispatch_total = slot_total(input_part, jnp.sum(weights, axis=1))
    slot_inputs = input_sum / dispatch_total[:, None]
    slot_inputs_b = slot_inputs.astype(jnp.bfloat16)
    dispatch = weights / dispatch_total[:, None]
    combine = weights / combine_total[None, :]
    grad_out_part = jnp.dot(
        combine.astype(jnp.bfloat16), out_grad, preferred_element_type=jnp.float32
    )
    experts_here = first_mixing.shape[0]
    model_width = tokens.shape[1]
    slots_each = slot_inputs_b.shape[0] // experts_here
    grouped = slot_inputs_b.reshape(experts_here, slots_each, model_width)
    slot_out_part, first_flat, hidden, slopes, second_flat = jax.vmap(expert_forward)(
        grouped, first_mixing, first_blocks, second_mixing, second_blocks
    )
    slot_out_sum, slot_grad_sum = slot_total(
        slot_out_part.reshape(experts_here * slots_each, model_width), grad_out_part
    )
    slot_out_b = slot_out_sum.astype(jnp.bfloat16)
    slot_grad_b = slot_grad_sum.astype(jnp.bfloat16)
    combine_grad = jnp.einsum("sd,td->st", slot_out_b, out_grad, preferred_element_type=jnp.float32)
    combine_dot = token_total(jnp.sum(combine * combine_grad, axis=0))
    expert_results = jax.vmap(expert_backward)(
        grouped,
        slot_grad_b.reshape(experts_here, slots_each, model_width),
        first_flat,
        hidden,
        slopes,
        second_flat,
        first_mixing,
        first_blocks,
        second_mixing,
        second_blocks,
    )
    input_grad_part, first_mix_part, first_blocks_grad, second_mix_part, second_blocks_grad = (
        expert_results
    )
    input_grad, mixing_grads = slot_total(
        input_grad_part.reshape(experts_here * slots_each, model_width),
        jnp.stack([first_mix_part, second_mix_part]),
    )
    input_grad_b = input_grad.astype(jnp.bfloat16)
    dispatch_dot = jnp.sum(slot_inputs * input_grad, axis=1)
    dispatch_grad = jnp.einsum(
        "sd,td->st", input_grad_b, tokens, preferred_element_type=jnp.float32
    )
    logit_grad = combine * (combine_grad - combine_dot[None, :]) + dispatch * (
        dispatch_grad - dispatch_dot[:, None]
    )
    logit_grad_b = (logit_gain * logit_grad).astype(jnp.bfloat16)
    slot_unit_grad = lax.psum(
        jnp.dot(logit_grad_b, token_unit_b, preferred_element_type=jnp.float32), "seq"
    )
    grad_slots = unit_grad(slot_unit, slot_unit_grad, slot_norm)
    row_count = tokens.shape[0] // lax.axis_size("exp")
    grad_all, out_all, unit_all = (
        lax.all_gather(input_grad_b, "exp", axis=0, tiled=True),
        lax.all_gather(slot_out_b, "exp", axis=0, tiled=True),
        lax.all_gather(slot_unit_b, "exp", axis=0, tiled=True),
    )
    dispatch_all, dot_all = (
        lax.all_gather(dispatch_total, "exp", axis=0, tiled=True),
        lax.all_gather(dispatch_dot, "exp", axis=0, tiled=True),
    )
    first_row = lax.axis_index("exp") * row_count
    own_tokens = lax.dynamic_slice_in_dim(tokens, first_row, row_count, 0)
    own_grad = lax.dynamic_slice_in_dim(out_grad, first_row, row_count, 0)
    own_unit = lax.dynamic_slice_in_dim(token_unit, first_row, row_count, 0)
    own_unit_b = lax.dynamic_slice_in_dim(token_unit_b, first_row, row_count, 0)
    own_norm = lax.dynamic_slice_in_dim(token_norm, first_row, row_count, 0)
    own_total = lax.dynamic_slice_in_dim(combine_total, first_row, row_count, 0)
    own_dot = lax.dynamic_slice_in_dim(combine_dot, first_row, row_count, 0)
    own_weights = jnp.exp(
        logit_gain * jnp.dot(own_unit_b, unit_all.T, preferred_element_type=jnp.float32)
    )
    own_dispatch = own_weights / dispatch_all[None, :]
    own_combine = own_weights / own_total[:, None]
    own_combine_grad = jnp.dot(own_grad, out_all.T, preferred_element_type=jnp.float32)
    own_dispatch_grad = jnp.dot(own_tokens, grad_all.T, preferred_element_type=jnp.float32)
    own_logit = own_combine * (own_combine_grad - own_dot[:, None]) + own_dispatch * (
        own_dispatch_grad - dot_all[None, :]
    )
    own_logit_b = (logit_gain * own_logit).astype(jnp.bfloat16)
    direct = jnp.dot(
        own_dispatch.astype(jnp.bfloat16), grad_all, preferred_element_type=jnp.float32
    )
    through = jnp.dot(own_logit_b, unit_all, preferred_element_type=jnp.float32)
    grad_tokens = direct + unit_grad(own_unit, through, own_norm)
    return (
        grad_tokens,
        grad_slots,
        mixing_grads[0],
        first_blocks_grad,
        mixing_grads[1],
        second_blocks_grad,
    )


def solution(mesh):
    placed = (
        P("seq", None),
        P("seq", None),
        P("exp", None),
        P("exp", None, None, None),
        P("exp", None, None, "seq"),
        P("exp", None, None, None),
        P("exp", None, "seq", None),
    )
    return jax.shard_map(
        local,
        mesh=mesh,
        in_specs=placed,
        out_specs=(
            P(("seq", "exp"), None),
            P("exp", None),
            P("exp", None, None, None),
            P("exp", None, None, "seq"),
            P("exp", None, None, None),
            P("exp", None, "seq", None),
        ),
        check_vma=False,
    )
```

profile of v0, /device:TPU:1, one launch (start us, length us, event | category | flops | bytes accessed | tf_op | source)
XLA Modules:
  0.0 651.7 jit_solution(12688127571988477652)
XLA Ops:
  8.1 2.9 fusion
  11.2 5.0 convert_divide_fusion
  17.6 3.9 fusion.57
  23.0 71.5 %psum.64 = f32[1024]{0:T(1024)S(1)} all-reduce(f32[1024]{0:T(1024)S(1)} %get-tuple-element.19), channel_id=1, replica_groups=mesh['seq'=8,'exp'=32] {'exp'}, use_global_device_ids=true, to_apply=%region_5.0 | all-reduce | flops 1024 | bytes 8192 | tf_op jit(solution)/shard_map/psum | solution.py:105
  96.5 50.3 %all-reduce.16 = (bf16[32,1664]{1,0:T(8,128)(2,1)}, f32[32]{0:T(128)}) all-reduce(f32[32,1664]{1,0:T(8,128)} %fusion.41, f32[32]{0:T(128)} %get-tuple-element.18), channel_id=1, replica_groups=mesh['seq'=8,'exp'=32] {'seq'}, use_global_device_ids=true, to_apply=%region_6.0 | all-reduce | flops 53280 | bytes 319744 | tf_op jit(solution)/shard_map/psum | solution.py:109
  152.5 1.8 reshape.84
  166.3 2.3 reshape.85
  168.6 2.7 fusion.67
  172.8 2.0 fusion.2
  174.8 1.9 convolution_bitcast_fusion.3
  176.7 2.0 fusion.15
  180.2 2.9 fusion.68
  183.0 2.5 reshape.89
  185.6 2.2 convolution_bitcast_fusion.2
  191.8 1.8 reshape.91
  193.6 2.9 fusion.69
  198.3 2.2 convolution_bitcast_fusion
  200.4 1.9 reshape.90
  203.7 46.9 %all-reduce.17 = (bf16[32,1664]{1,0:T(8,128)(2,1)}, f32[2,2,4,4,4]{4,3,2,1,0:T(4,128)}) all-reduce(f32[32,1664]{1,0:T(8,128)} %reshape.92, f32[2,2,4,4,4]{4,3,2,1,0:T(4,128)} %pad_maximum_fusion), channel_id=1, replica_groups=mesh['seq'=8,'exp'=32] {'seq'}, use_global_device_ids=true, to_apply=%region_9.0 | all-reduce | flops 53504 | bytes 321536 | tf_op jit(solution)/shard_map/psum | solution.py:109
  250.7 3.2 multiply_reduce_fusion.3
  253.9 51.0 %all-reduce.13.cloned.1.call-done = f32[32,1664]{1,0:T(8,128)} async-done(((f32[32,1664]{1,0:T(8,128)}), f32[32,1664]{1,0:T(8,128)}) %all-reduce.13.cloned.1.call-update) | async-done | bytes 213008 | tf_op jit(solution)/shard_map/psum | solution.py:109
  304.9 1.9 multiply_reduce_fusion.2
  307.3 132.5 %all-reduce.2 = (f32[1024]{0:T(1024)}, f32[1024]{0:T(1024)}, f32[1024]{0:T(1024)S(1)}) all-reduce(f32[1024]{0:T(1024)} %get-tuple-element.34, f32[1024]{0:T(1024)S(1)} %dynamic-update-slice.1, f32[1024]{0:T(1024)S(1)} %copy-done.14), channel_id=1, replica_groups=mesh['seq'=8,'exp'=32] {'exp'}, use_global_device_ids=true, to_apply=%region_11.0 | all-reduce | flops 3072 | bytes 24576 | tf_op jit(solution)/shard_map/psum | solution.py:105
  439.8 5.5 fusion.16
  451.6 1.8 convolution_convert_fusion
  454.7 89.4 %all-reduce.15.cloned.1.call-done = f32[32,1664]{1,0:T(8,128)} async-done(((f32[32,1664]{1,0:T(8,128)}), f32[32,1664]{1,0:T(8,128)}) %all-reduce.15.cloned.1.call-update) | async-done | bytes 213008 | tf_op jit(solution)/shard_map/psum | solution.py:183
  547.0 3.2 fusion.12
  550.2 22.4 %all-gather.8.cloned.1.call-done = bf16[1024,1664]{1,0:T(8,128)(2,1)} async-done(((bf16[32,1664]{1,0:T(8,128)(2,1)}), bf16[1024,1664]{1,0:T(8,128)(2,1)}) %all-gather.8.cloned.1.call-update) | async-done | bytes 3407888 | tf_op jit(solution)/shard_map/all_gather | solution.py:190
  572.6 3.7 fusion.10
  576.3 59.0 %all-gather.6.cloned.1.call-done = bf16[1024,1664]{1,0:T(8,128)(2,1)} async-done(((bf16[32,1664]{1,0:T(8,128)(2,1)}), bf16[1024,1664]{1,0:T(8,128)(2,1)}) %all-gather.6.cloned.1.call-update) | async-done | bytes 3407888 | tf_op jit(solution)/shard_map/all_gather | solution.py:189
  635.3 5.5 multiply_reduce_fusion.1
  640.8 3.5 convolution_add_fusion
  (91 shorter events, 43.3 us)
Async XLA Ops:
  8.0 87.1 %copy-start = (bf16[1024,1664]{1,0:T(8,128)(2,1)S(1)}, bf16[1024,1664]{1,0:T(8,128)(2,1)}, u32[]{:S(2)}) copy-start(bf16[1024,1664]{1,0:T(8,128)(2,1)} %param.8) | copy-start | bytes 10223620
  8.0 152.4 %all-reduce.11.cloned.1.call-start = ((), (), s32[]{:S(2)}) async-start(), calls=%async_computation.1 | async-start | bytes 425984 | tf_op jit(solution)/shard_map/psum | solution.py:109
  8.1 3.1 copy-start.1
  11.2 5.0 copy-start.13
  11.2 5.0 copy-start.5
  16.3 0.6 copy-start.16
  17.6 3.9 copy-start.2
  23.0 282.0 %all-reduce.13.cloned.1.call-start = ((), (), s32[]{:S(2)}) async-start(), calls=%async_computation.2 | async-start | bytes 425984 | tf_op jit(solution)/shard_map/psum | solution.py:109
  94.5 0.6 copy-start.10
  96.5 59.4 %copy-start.9 = (f32[2,4,4,4]{3,2,1,0:T(4,128)S(1)}, f32[2,4,4,4]{3,2,1,0:T(4,128)}, u32[]{:S(2)}) copy-start(f32[2,4,4,4]{3,2,1,0:T(4,128)} %param.10) | copy-start | bytes 1540
  148.5 2.9 copy-start.7
  150.2 1.2 copy-start.3
  165.2 7.6 %copy-start.15 = (f32[2,4,4,4]{3,2,1,0:T(4,128)S(1)}, f32[2,4,4,4]{3,2,1,0:T(4,128)}, u32[]{:S(2)}) copy-start(f32[2,4,4,4]{3,2,1,0:T(4,128)} %param.12) | copy-start | bytes 1540
  202.3 341.8 %all-reduce.15.cloned.1.call-start = ((), (), s32[]{:S(2)}) async-start(), calls=%async_computation.5 | async-start | bytes 425984 | tf_op jit(solution)/shard_map/psum | solution.py:183
  203.7 101.2 %copy-start.18 = (f32[32]{0:T(128)S(1)}, f32[32]{0:T(128)}, u32[]{:S(2)}) copy-start(f32[32]{0:T(128)} %get-tuple-element.26) | copy-start | bytes 388
  203.7 103.6 %copy-start.14 = (f32[1024]{0:T(1024)S(1)}, f32[1024]{0:T(1024)}, u32[]{:S(2)}) copy-start(f32[1024]{0:T(1024)} %dynamic-update-slice) | copy-start | bytes 12292
  203.7 236.1 %copy-start.11 = (f32[1024]{0:T(1024)S(1)}, f32[1024]{0:T(1024)}, u32[]{:S(2)}) copy-start(f32[1024]{0:T(1024)} %copy-done.10) | copy-start | bytes 12292
  306.8 0.5 copy-start.20
  445.3 101.7 %all-gather.4.cloned.1.call-start = ((), (), s32[]{:S(2)}) async-start(), calls=%async_computation | async-start | bytes 3514368 | tf_op jit(solution)/shard_map/all_gather | solution.py:191
  445.9 126.6 %all-gather.8.cloned.1.call-start = ((), (), s32[]{:S(2)}) async-start(), calls=%async_computation.4 | async-start | bytes 3514368 | tf_op jit(solution)/shard_map/all_gather | solution.py:190
  446.5 188.8 %all-gather.6.cloned.1.call-start = ((), (), s32[]{:S(2)}) async-start(), calls=%async_computation.3 | async-start | bytes 3514368 | tf_op jit(solution)/shard_map/all_gather | solution.py:189
  447.1 3.9 copy-start.12
  447.1 4.5 copy-start.4
  447.1 4.5 copy-start.8
  448.0 96.1 %copy-start.6 = (bf16[32,1664]{1,0:T(8,128)(2,1)S(1)}, bf16[32,1664]{1,0:T(8,128)(2,1)}, u32[]{:S(2)}) copy-start(bf16[32,1664]{1,0:T(8,128)(2,1)} %param.9) | copy-start | bytes 319492
  448.0 96.1 %copy-start.17 = (f32[32]{0:T(128)S(1)}, f32[32]{0:T(128)}, u32[]{:S(2)}) copy-start(f32[32]{0:T(128)} %copy-done.16) | copy-start | bytes 388
  547.0 88.3 %copy-start.19 = (f32[1024]{0:T(1024)S(1)}, f32[1024]{0:T(1024)}, u32[]{:S(2)}) copy-start(f32[1024]{0:T(1024)} %get-tuple-element.21) | copy-start | bytes 12292
Sparse Core Ops, SparseCore 0:
  23.1 102.7 all-reduce.10
  202.4 102.4 all-reduce.12
  445.5 98.6 all-reduce.14
Sparse Core Ops, SparseCore 1:
  447.7 62.2 all-gather.3
  511.8 60.7 all-gather.7
  574.3 61.0 all-gather.5
where the time goes:
time: 653 us; the launch traced here: 652 us
  blocking collectives  301 us (46%)
  waiting for transfers between devices  223 us (34%)
  matrix products  55.9 us (9%)
  local copies, waits for them, and re-layouts  38.1 us (6%)
  other arithmetic  16.5 us (3%)
  between operations  16.3 us (2%)
    psum x2, blocking collectives, token_total(): return lax.psum(partial_sums, 'exp')  204 us
    psum x2, blocking collectives, slot_total(): return lax.psum((first_part, second_part), 'seq')  97.3 us
    psum x1, waiting for transfers between devices, local(): lax.psum(jnp.dot(logit_grad_b, token_unit_b, preferred_element_type=jnp.f...  89.4 us
    all_gather x1, waiting for transfers between devices, local(): lax.all_gather(input_grad_b, 'exp', axis=0, tiled=True)  59 us
    psum x2, waiting for transfers between devices, slot_total(): return lax.psum((first_part, second_part), 'seq')  51 us
    all_gather x1, waiting for transfers between devices, local(): lax.all_gather(slot_out_b, 'exp', axis=0, tiled=True)  22.4 us
  transfers between devices with their start and end apart: 6, of which 4 were waited for; matrix products, arithmetic and copies ran while one was open for 5% of the time, Pallas kernels for 0%

commit v1 on v0

--- a/solution.py
+++ b/solution.py
@@ -180,8 +180,11 @@
         dispatch_grad - dispatch_dot[:, None]
     )
     logit_grad_b = (logit_gain * logit_grad).astype(jnp.bfloat16)
-    slot_unit_grad = lax.psum(
-        jnp.dot(logit_grad_b, token_unit_b, preferred_element_type=jnp.float32), "seq"
+    slot_unit_grad = jnp.sum(
+        lax.all_gather(
+            jnp.dot(logit_grad_b, token_unit_b, preferred_element_type=jnp.float32), "seq"
+        ),
+        axis=0,
     )
     grad_slots = unit_grad(slot_unit, slot_unit_grad, slot_norm)
     row_count = tokens.shape[0] // lax.axis_size("exp")

time: 653 us -> 717 us (1.098)
  waiting for transfers between devices: 223 us -> 287 us
    psum x1 -> x0, waiting for transfers between devices: 89.4 us -> none  [local(): lax.psum(jnp.dot(logit_grad_b, token_unit_b, preferred_element_type=jnp.f...]
    all_gather x0 -> x1, waiting for transfers between devices: none -> 59.4 us  [local(): lax.all_gather(jnp.dot(logit_grad_b, token_unit_b, preferred_element_type...]
    all_gather x1, waiting for transfers between devices: 0.01 us -> 56 us  [local(): lax.all_gather(slot_unit_b, 'exp', axis=0, tiled=True)]
    all_gather x1, waiting for transfers between devices: 22.4 us -> 59.5 us  [local(): lax.all_gather(slot_out_b, 'exp', axis=0, tiled=True)]
  transfers between devices with their start and end apart: 6 -> 6, of which waited for: 4 -> 5; matrix products, arithmetic and copies ran while one was open for 5% -> 5% of each run, Pallas kernels for 0% -> 0%
where the time goes in v1:
time: 717 us; the launch traced here: 715 us
  blocking collectives  300 us (42%)
  waiting for transfers between devices  287 us (40%)
  matrix products  55.9 us (8%)
  local copies, waits for them, and re-layouts  38.2 us (5%)
  other arithmetic  18.7 us (3%)
  between operations  14.9 us (2%)
    psum x2, blocking collectives, token_total(): return lax.psum(partial_sums, 'exp')  204 us
    psum x2, blocking collectives, slot_total(): return lax.psum((first_part, second_part), 'seq')  96.2 us
    all_gather x1, waiting for transfers between devices, local(): lax.all_gather(slot_out_b, 'exp', axis=0, tiled=True)  59.5 us
    all_gather x1, waiting for transfers between devices, local(): lax.all_gather(jnp.dot(logit_grad_b, token_unit_b, preferred_element_type...  59.4 us
    all_gather x1, waiting for transfers between devices, local(): lax.all_gather(input_grad_b, 'exp', axis=0, tiled=True)  58.9 us
    all_gather x1, waiting for transfers between devices, local(): lax.all_gather(slot_unit_b, 'exp', axis=0, tiled=True)  56 us
    psum x2, waiting for transfers between devices, slot_total(): return lax.psum((first_part, second_part), 'seq')  51.7 us
  transfers between devices with their start and end apart: 6, of which 5 were waited for; matrix products, arithmetic and copies ran while one was open for 5% of the time, Pallas kernels for 0%

profile of v1, /device:TPU:1, one launch (start us, length us, event | category | flops | bytes accessed | tf_op | source)
XLA Modules:
  0.0 715.2 jit_solution(1411290285244020100)
XLA Ops:
  7.2 2.9 fusion
  10.4 5.0 convert_divide_fusion
  16.8 3.9 fusion.57
  22.2 71.5 %psum.57 = f32[1024]{0:T(1024)S(1)} all-reduce(f32[1024]{0:T(1024)S(1)} %get-tuple-element.19), channel_id=1, replica_groups=mesh['seq'=8,'exp'=32] {'exp'}, use_global_device_ids=true, to_apply=%region_5.0 | all-reduce | flops 1024 | bytes 8192 | tf_op jit(solution)/shard_map/psum | solution.py:105
  95.6 50.6 %all-reduce.13 = (bf16[32,1664]{1,0:T(8,128)(2,1)}, f32[32]{0:T(128)}) all-reduce(f32[32,1664]{1,0:T(8,128)} %fusion.41, f32[32]{0:T(128)} %get-tuple-element.18), channel_id=1, replica_groups=mesh['seq'=8,'exp'=32] {'seq'}, use_global_device_ids=true, to_apply=%region_6.0 | all-reduce | flops 53280 | bytes 319744 | tf_op jit(solution)/shard_map/psum | solution.py:109
  165.8 2.3 reshape.85
  168.1 2.7 fusion.67
  172.3 2.0 fusion.2
  174.3 1.9 convolution_bitcast_fusion.3
  176.2 2.0 fusion.15
  179.7 2.9 fusion.68
  182.5 2.5 reshape.89
  185.1 2.2 convolution_bitcast_fusion.2
  193.1 2.9 fusion.69
  197.8 2.2 convolution_bitcast_fusion
  199.9 1.9 reshape.90
  203.2 45.6 %all-reduce.14 = (bf16[32,1664]{1,0:T(8,128)(2,1)}, f32[2,2,4,4,4]{4,3,2,1,0:T(4,128)}) all-reduce(f32[32,1664]{1,0:T(8,128)} %reshape.92, f32[2,2,4,4,4]{4,3,2,1,0:T(4,128)} %pad_maximum_fusion), channel_id=1, replica_groups=mesh['seq'=8,'exp'=32] {'seq'}, use_global_device_ids=true, to_apply=%region_9.0 | all-reduce | flops 53504 | bytes 321536 | tf_op jit(solution)/shard_map/psum | solution.py:109
  248.8 3.3 multiply_reduce_fusion.3
  252.1 51.7 %all-reduce.12.cloned.1.call-done = f32[32,1664]{1,0:T(8,128)} async-done(((f32[32,1664]{1,0:T(8,128)}), f32[32,1664]{1,0:T(8,128)}) %all-reduce.12.cloned.1.call-update) | async-done | bytes 213008 | tf_op jit(solution)/shard_map/psum | solution.py:109
  303.7 1.9 multiply_reduce_fusion.2
  306.2 132.5 %all-reduce.2 = (f32[1024]{0:T(1024)}, f32[1024]{0:T(1024)}, f32[1024]{0:T(1024)S(1)}) all-reduce(f32[1024]{0:T(1024)} %get-tuple-element.34, f32[1024]{0:T(1024)S(1)} %dynamic-update-slice.1, f32[1024]{0:T(1024)S(1)} %copy-done.14), channel_id=1, replica_groups=mesh['seq'=8,'exp'=32] {'exp'}, use_global_device_ids=true, to_apply=%region_11.0 | all-reduce | flops 3072 | bytes 24576 | tf_op jit(solution)/shard_map/psum | solution.py:105
  438.7 5.5 fusion.16
  450.4 1.8 convolution_convert_fusion
  453.6 59.4 %all-gather.12.cloned.1.call-done = f32[256,1664]{1,0:T(8,128)} async-done(((f32[32,1664]{1,0:T(8,128)}), f32[256,1664]{1,0:T(8,128)}) %all-gather.12.cloned.1.call-update) | async-done | bytes 1703952 | tf_op jit(solution)/shard_map/all_gather | solution.py:184
  513.0 2.2 reduce_sum.88
  518.1 56.0 %all-gather.6.cloned.1.call-done = bf16[1024,1664]{1,0:T(8,128)(2,1)} async-done(((bf16[32,1664]{1,0:T(8,128)(2,1)}), bf16[1024,1664]{1,0:T(8,128)(2,1)}) %all-gather.6.cloned.1.call-update) | async-done | bytes 3407888 | tf_op jit(solution)/shard_map/all_gather | solution.py:194
  574.1 3.1 fusion.12
  577.3 59.5 %all-gather.10.cloned.1.call-done = bf16[1024,1664]{1,0:T(8,128)(2,1)} async-done(((bf16[32,1664]{1,0:T(8,128)(2,1)}), bf16[1024,1664]{1,0:T(8,128)(2,1)}) %all-gather.10.cloned.1.call-update) | async-done | bytes 3407888 | tf_op jit(solution)/shard_map/all_gather | solution.py:193
  636.8 3.7 fusion.10
  640.5 58.9 %all-gather.8.cloned.1.call-done = bf16[1024,1664]{1,0:T(8,128)(2,1)} async-done(((bf16[32,1664]{1,0:T(8,128)(2,1)}), bf16[1024,1664]{1,0:T(8,128)(2,1)}) %all-gather.8.cloned.1.call-update) | async-done | bytes 3407888 | tf_op jit(solution)/shard_map/all_gather | solution.py:192
  699.4 5.5 multiply_reduce_fusion.1
  704.9 3.5 convolution_add_fusion
  (92 shorter events, 47.0 us)
Async XLA Ops:
  7.2 87.1 %copy-start = (bf16[1024,1664]{1,0:T(8,128)(2,1)S(1)}, bf16[1024,1664]{1,0:T(8,128)(2,1)}, u32[]{:S(2)}) copy-start(bf16[1024,1664]{1,0:T(8,128)(2,1)} %param.8) | copy-start | bytes 10223620
  7.2 152.7 %all-reduce.10.cloned.1.call-start = ((), (), s32[]{:S(2)}) async-start(), calls=%async_computation.1 | async-start | bytes 425984 | tf_op jit(solution)/shard_map/psum | solution.py:109
  7.2 3.1 copy-start.1
  10.4 5.0 copy-start.13
  10.4 5.0 copy-start.5
  15.5 0.6 copy-start.16
  16.8 3.9 copy-start.2
  22.1 281.6 %all-reduce.12.cloned.1.call-start = ((), (), s32[]{:S(2)}) async-start(), calls=%async_computation.2 | async-start | bytes 425984 | tf_op jit(solution)/shard_map/psum | solution.py:109
  93.7 0.6 copy-start.10
  95.6 59.7 %copy-start.9 = (f32[2,4,4,4]{3,2,1,0:T(4,128)S(1)}, f32[2,4,4,4]{3,2,1,0:T(4,128)}, u32[]{:S(2)}) copy-start(f32[2,4,4,4]{3,2,1,0:T(4,128)} %param.10) | copy-start | bytes 1540
  148.0 2.9 copy-start.7
  149.7 1.2 copy-start.3
  164.7 7.6 %copy-start.15 = (f32[2,4,4,4]{3,2,1,0:T(4,128)S(1)}, f32[2,4,4,4]{3,2,1,0:T(4,128)}, u32[]{:S(2)}) copy-start(f32[2,4,4,4]{3,2,1,0:T(4,128)} %param.12) | copy-start | bytes 1540
  201.8 311.1 %all-gather.12.cloned.1.call-start = ((), (), s32[]{:S(2)}) async-start(), calls=%async_computation.5 | async-start | bytes 1916928 | tf_op jit(solution)/shard_map/all_gather | solution.py:184
  203.2 100.5 %copy-start.18 = (f32[32]{0:T(128)S(1)}, f32[32]{0:T(128)}, u32[]{:S(2)}) copy-start(f32[32]{0:T(128)} %get-tuple-element.26) | copy-start | bytes 388
  203.2 102.9 %copy-start.14 = (f32[1024]{0:T(1024)S(1)}, f32[1024]{0:T(1024)}, u32[]{:S(2)}) copy-start(f32[1024]{0:T(1024)} %dynamic-update-slice) | copy-start | bytes 12292
  203.2 235.4 %copy-start.11 = (f32[1024]{0:T(1024)S(1)}, f32[1024]{0:T(1024)}, u32[]{:S(2)}) copy-start(f32[1024]{0:T(1024)} %copy-done.10) | copy-start | bytes 12292
  305.7 0.5 copy-start.20
  444.2 130.0 %all-gather.6.cloned.1.call-start = ((), (), s32[]{:S(2)}) async-start(), calls=%async_computation | async-start | bytes 3514368 | tf_op jit(solution)/shard_map/all_gather | solution.py:194
  444.8 192.0 %all-gather.10.cloned.1.call-start = ((), (), s32[]{:S(2)}) async-start(), calls=%async_computation.4 | async-start | bytes 3514368 | tf_op jit(solution)/shard_map/all_gather | solution.py:193
  445.3 254.1 %all-gather.8.cloned.1.call-start = ((), (), s32[]{:S(2)}) async-start(), calls=%async_computation.3 | async-start | bytes 3514368 | tf_op jit(solution)/shard_map/all_gather | solution.py:192
  445.9 3.9 copy-start.12
  445.9 4.5 copy-start.4
  445.9 4.5 copy-start.8
  448.5 66.7 %copy-start.6 = (bf16[32,1664]{1,0:T(8,128)(2,1)S(1)}, bf16[32,1664]{1,0:T(8,128)(2,1)}, u32[]{:S(2)}) copy-start(bf16[32,1664]{1,0:T(8,128)(2,1)} %param.9) | copy-start | bytes 319492
  448.5 66.7 %copy-start.17 = (f32[32]{0:T(128)S(1)}, f32[32]{0:T(128)}, u32[]{:S(2)}) copy-start(f32[32]{0:T(128)} %copy-done.16) | copy-start | bytes 388
  518.1 181.3 %copy-start.19 = (f32[1024]{0:T(1024)S(1)}, f32[1024]{0:T(1024)}, u32[]{:S(2)}) copy-start(f32[1024]{0:T(1024)} %get-tuple-element.21) | copy-start | bytes 12292
Sparse Core Ops, SparseCore 0:
  22.3 102.7 all-reduce.9
  202.0 101.7 all-reduce.11
  444.3 68.6 all-gather.11
  514.7 59.3 all-gather.5
  575.8 60.9 all-gather.9
  638.5 60.8 all-gather.7
